TPU v7x, 256 devices: a whole 4x4x8 slice. The times are simulated.
256 devices in a mesh: ev: 64 (over y, z_lo, x, core), sys: 4 (over z_hi).
Axes of the slice: x: 4, y: 4, z: 8 (z_hi: 4, z_lo: 2; z = z_hi * 2 + z_lo), core: 2. Of those that a mesh axis runs over, the one named last changes fastest.
Arguments:
- observables: bfloat16 [32768, 512], P('ev'), may hold values from -6 to 6
- selection: int32 [32768, 512], P('ev'), may hold values 0 or 1
- base_weight: float32 [32768], P('ev'), may hold values from 0.05 to 0.5
- category: int32 [32768], P('ev'), may hold values from 0 to 63
- bin_number: int32 [32768], P('ev'), may hold values from 0 to 255
- response: bfloat16 [512, 512], P(None, 'sys'), may hold values from -0.25 to 0.25
- nuisance_pulls: float32 [256], P('sys'), may hold values from -2 to 2
Outputs:
- templates: float32 [64, 512, 256], P('ev', 'sys')
- expected: float32 [64, 256], P('ev')
All inputs are finite; a program needn't handle non-finite values. No bound on the sum of `selection` on one device may be relied on, other than what follows from the above.
Results may differ from a plain program's by a relative error of at most 0.0003.
Values sent between devices are 32-bit elements; how exact they have to be, the bound alone decides.
A program may use at most 64 MiB of HBM per device.

v0:
```python
import jax
import jax.numpy as jnp
from jax import lax
from jax.sharding import PartitionSpec as P

C = 64
B = 256


def channel_onehot(category, row_start, row_count):
    channels = row_start + jnp.arange(row_count, dtype=jnp.int32)
    return (category[:, None] == channels[None, :]).astype(jnp.float32)


def bin_onehot(bin_number):
    return (bin_number[:, None] == jnp.arange(B, dtype=jnp.int32)[None, :]).astype(jnp.float32)


def contract_rows(stacked, onehot):
    return lax.dot_general(
        stacked,
        onehot,
        (((0,), (0,)), ((), ())),
        precision=lax.Precision.HIGHEST,
        preferred_element_type=jnp.float32,
    )


def over_blocks(events, one_block, initial):
    block_rows = min(512, events)
    full_blocks = events // block_rows

    def add_block(block_index, accumulated):
        return accumulated + one_block(block_index * block_rows, block_rows)

    accumulated = lax.fori_loop(0, full_blocks, add_block, initial)
    return accumulated


def fill_variations(variation_weight, category, bin_number, chan_start, chan_count, var_count):
    events = variation_weight.shape[0]

    def one_block(lower, rows):
        in_channel = channel_onehot(category, chan_start, chan_count)
        onehot = bin_onehot(bin_number)
        stacked = (variation_weight[:, :, None] * in_channel[:, None, :]).reshape(
            rows, var_count * chan_count
        )
        return contract_rows(stacked, onehot)

    return over_blocks(events, one_block, jnp.zeros((chan_count * var_count, B), jnp.float32))


def fill_nominal(nominal_weight, category, bin_number, chan_start, chan_count):
    events = nominal_weight.shape[0]

    def one_block(lower, rows):
        weighted = channel_onehot(category, chan_start, chan_count) * nominal_weight[:, None]
        return contract_rows(weighted, bin_onehot(bin_number))

    return over_blocks(events, one_block, jnp.zeros((chan_count, B), jnp.float32))


def local(observables, selection, base_weight, category, bin_number, response, nuisance_pulls):
    masked = observables * selection.astype(jnp.bfloat16)
    log_shift = jnp.dot(masked, response, preferred_element_type=jnp.float32)
    variation_weight = base_weight[:, None] * jnp.exp(0.2 * log_shift)
    var_local = variation_weight.shape[1]
    ev_count = lax.axis_size("ev")
    chan_local = C // ev_count
    position = lax.axis_index("ev")
    kept_rows = var_local // ev_count
    summed = fill_variations(
        variation_weight, category, bin_number, 0, C, kept_rows * lax.axis_size("ev")
    )
    received = lax.psum_scatter(
        summed.reshape(kept_rows * lax.axis_size("ev"), C * B),
        "ev",
        scatter_dimension=0,
        tiled=True,
    )
    received = received.reshape(kept_rows, C, B)
    moved = lax.all_to_all(received, "ev", split_axis=1, concat_axis=0, tiled=True)
    templates = jnp.transpose(moved, (1, 0, 2))
    whole_nominal = lax.psum(fill_nominal(base_weight, category, bin_number, 0, C), "ev")
    nominal = lax.dynamic_slice_in_dim(whole_nominal, position * chan_local, chan_local, 0)
    upward = templates[:, 0::2, :]
    downward = templates[:, 1::2, :]
    pull_col = nuisance_pulls[None, :, None]
    nominal_col = nominal[:, None, :]
    changes = jnp.where(
        pull_col >= 0.0, pull_col * (upward - nominal_col), pull_col * (nominal_col - downward)
    )
    change_total = lax.psum(jnp.sum(changes, axis=1), "sys")
    expected = nominal + change_total
    return (templates, expected)


def solution(mesh):
    placed = (P("ev", None), P("ev", None), P("ev"), P("ev"), P("ev"), P(None, "sys"), P("sys"))
    return jax.shard_map(
        local,
        mesh=mesh,
        in_specs=placed,
        out_specs=(P("ev", "sys", None), P("ev", None)),
        check_vma=False,
    )
```

profile of v0, /device:TPU:1, one launch (start us, length us, event | category | flops | bytes accessed | tf_op | source)
XLA Modules:
  0.0 649.7 jit_solution(8411119167193394503)
XLA Ops:
  7.2 0.0 copy-start
  7.2 0.0 copy-start.2
  7.2 0.0 all-reduce.4.cloned.1.call-start
  7.2 0.7 fusion.9
  7.9 0.1 copy-done
  8.1 1.7 fusion.1
  9.8 0.1 copy.14
  9.9 1.7 fusion.2
  11.6 2.5 broadcast_multiply_fusion
  14.1 0.0 copy-done.2
  14.1 10.4 %fusion.3 = f32[8192,256]{1,0:T(8,128)} fusion(f32[512,8192]{0,1:T(8,128)S(1)} %bitcast.12, s32[512]{0:T(512)S(1)} %copy-done.2), kind=kOutput, calls=%fused_computation.6 | convolution fusion | flops 12885032960 | bytes 25167872 | tf_op jit(solution)/shard_map/while/body/eval_jaxpr/dot_general | solution.py:20
  24.5 0.0 copy-start.4
  24.5 0.0 copy-start.3
  24.5 9.4 %reshape.48 = f32[128,16384]{1,0:T(8,128)} reshape(f32[8192,256]{1,0:T(8,128)} %fusion.3) | data formatting | bytes 16777216 | tf_op jit(solution)/shard_map/reshape | solution.py:77
  33.9 0.0 all-reduce.4.cloned.1.call-update
  34.0 0.0 copy-done.4
  34.0 0.6 dynamic-slice
  35.2 578.4 %all-reduce.4.cloned.1.call-done = (f32[128,16384]{1,0:T(8,128)}, f32[64,256]{1,0:T(8,128)}) async-done(((f32[128,16384]{1,0:T(8,128)}, f32[64,256]{1,0:T(8,128)}), (f32[128,16384]{1,0:T(8,128)}, f32[64,256]{1,0:T(8,128)})) %all-reduce.4.cloned.1.call-update) | async-done | bytes 8454160
  613.7 1.7 constant_dynamic-slice_fusion
  615.4 6.9 %all-to-all-start = ((f32[2,64,256]{2,0,1:T(2,128)}), f32[2,64,256]{2,0,1:T(2,128)S(1)}, u32[]{:S(2)}, u32[]{:S(2)}) async-start(f32[2,64,256]{2,0,1:T(2,128)} %bitcast.1), calls=%async_computation | async-start | bytes 262144 | tf_op jit(solution)/shard_map/all_to_all | solution.py:83
  622.3 0.0 copy-done.3
  622.3 0.7 constant_dynamic-slice_fusion.1
  623.0 7.9 %all-to-all-done = f32[2,64,256]{2,0,1:T(2,128)S(1)} async-done(((f32[2,64,256]{2,0,1:T(2,128)}), f32[2,64,256]{2,0,1:T(2,128)S(1)}, u32[]{:S(2)}, u32[]{:S(2)}) %all-to-all-start) | async-done | bytes 131104 | tf_op jit(solution)/shard_map/all_to_all | solution.py:83
  630.9 0.1 transpose.13
  631.0 0.0 copy-start.1
  631.0 0.1 select_reduce_fusion
  631.1 10.5 %psum.15 = f32[1,256]{1,0:T(1,128)S(1)} all-reduce(f32[1,256]{1,0:T(1,128)S(1)} %bitcast.15), channel_id=1, replica_groups=mesh['ev'=64,'sys'=4] {'sys'}, use_global_device_ids=true, to_apply=%region_3.0 | all-reduce | flops 256 | bytes 2048 | tf_op jit(solution)/shard_map/psum | solution.py:94
  641.6 1.3 fusion.16
  642.9 0.0 copy-done.1
  (3 shorter events, 0.1 us)
Async XLA Ops:
  7.2 0.9 copy-start
  7.2 6.9 %copy-start.2 = (s32[512]{0:T(512)S(1)}, s32[512]{0:T(512)}, u32[]{:S(2)}) copy-start(s32[512]{0:T(512)} %param.11) | copy-start | bytes 6148
  7.2 606.5 %all-reduce.4.cloned.1.call-start = ((), (), s32[]{:S(2)}) async-start(), calls=%async_computation.1 | async-start | bytes 16908288
  24.5 9.4 %copy-start.4 = (u32[256]{0:T(256)S(1)}, u32[256]{0:T(256)}, u32[]{:S(2)}) copy-start(u32[256]{0:T(256)} %constant.26) | copy-start | bytes 3076
  24.5 597.7 %copy-start.3 = (f32[64]{0:T(128)S(1)}, f32[64]{0:T(128)}, u32[]{:S(2)}) copy-start(f32[64]{0:T(128)} %param.13) | copy-start | bytes 772
  615.4 15.5 %all-to-all-start = ((f32[2,64,256]{2,0,1:T(2,128)}), f32[2,64,256]{2,0,1:T(2,128)S(1)}, u32[]{:S(2)}, u32[]{:S(2)}) async-start(f32[2,64,256]{2,0,1:T(2,128)} %bitcast.1), calls=%async_computation | async-start | bytes 262144 | tf_op jit(solution)/shard_map/all_to_all | solution.py:83
  631.0 11.9 %copy-start.1 = (f32[1,128,256]{2,1,0:T(8,128)}, f32[1,128,256]{2,1,0:T(8,128)S(1)}, u32[]{:S(2)}) copy-start(f32[1,128,256]{2,1,0:T(8,128)S(1)} %transpose.13) | copy-start | bytes 393220
Sparse Core Ops, SparseCore 0:
  34.1 579.5 all-reduce.3
where the time goes:
time: 650 us
  waiting for transfers between devices  586 us (90%)
  between operations  14.8 us (2%)
  matrix products  13.8 us (2%)
  local copies, waits for them, and re-layouts  12.9 us (2%)
  blocking collectives  10.5 us (2%)
  starting transfers between devices  6.9 us (1%)
    unnamed x2, waiting for transfers between devices  578 us
  transfers between devices with their start and end apart: 2, of which 2 were waited for; matrix products, arithmetic and copies ran while one was open for 0% of the time, Pallas kernels for 0%

commit v1 on v0

v1 whole, which is shorter than its diff:
```python
import functools

import jax
import jax.numpy as jnp
from jax import lax
from jax.experimental import pallas as pl
from jax.experimental.pallas import tpu as pltpu
from jax.sharding import PartitionSpec as P

B = 256
K = 24
U_LANE = 32
N_LANE = 64
MESH = pl.DeviceIdType.MESH
F32 = jnp.float32
BF16 = jnp.bfloat16


def iota(shape, dim):
    return lax.broadcasted_iota(jnp.int32, shape, dim)


def onehot(mask):
    return jnp.where(mask, 1.0, 0.0).astype(BF16)


def parts(x, count):
    out = []
    for _ in range(count):
        piece = x.astype(BF16)
        out.append(piece)
        x = x - piece.astype(F32)
    return out


def dot(a, b):
    return jnp.dot(a, b, preferred_element_type=F32)


def dot_nt(a, b):
    return lax.dot_general(a, b, (((1,), (1,)), ((), ())), preferred_element_type=F32)


def exchange(n_ev, n_sys, later, *refs):
    if later:
        round_ref, *refs = refs
    (
        obs_hbm, sel_hbm, base_ref, cat_ref, bin_ref, resp_ref, pull_ref,
        hist_ref, expected_ref, most_ref,
        obs, sel, weight, send, recv, meta, meta_in, u_all,
        load_sem, u_send_sem, u_recv_sem, send_sem, recv_sem, meta_send_sem, meta_recv_sem,
    ) = refs
    events, features = obs.shape
    variations = weight.shape[1]
    me, my_sys = lax.axis_index("ev"), lax.axis_index("sys")
    steps = 4
    rows = events // steps

    loads = []
    for i in range(steps):
        part = pl.ds(i * rows, rows)
        loads.append((
            pltpu.make_async_copy(obs_hbm.at[part], obs.at[part], load_sem.at[0, i]),
            pltpu.make_async_copy(sel_hbm.at[part], sel.at[part], load_sem.at[1, i]),
        ))
        for load in loads[-1]:
            load.start()

    barrier = pltpu.get_barrier_semaphore()

    def greet(d, carry):
        pl.semaphore_signal(
            barrier, inc=1, device_id={"ev": lax.rem(me + d, n_ev)}, device_id_type=MESH
        )
        return carry

    lax.fori_loop(1, n_ev, greet, 0)
    for q in range(1, n_sys):
        pl.semaphore_signal(
            barrier, inc=1, device_id={"sys": lax.rem(my_sys + q, n_sys)}, device_id_type=MESH
        )

    cat = cat_ref[...]
    in_channel = iota((n_ev, events), 0) == cat
    before = onehot(iota((events, events), 0) < iota((events, events), 1))
    ahead = dot(onehot(in_channel), before)
    rank = jnp.sum(jnp.where(in_channel, ahead, 0.0), axis=0, keepdims=True)
    most = jnp.max(rank, axis=1, keepdims=True) + 1.0
    rank = rank.astype(jnp.int32)
    if later:
        rank = rank - round_ref[0] * K
    kept = jnp.logical_and(rank >= 0, rank < K)
    slot = jnp.where(kept, cat * K + rank, -1)
    rank = jnp.where(kept, rank, -1)

    base = base_ref[...]
    base_col = jnp.broadcast_to(base, (variations, events)).T
    for i in range(steps):
        part = pl.ds(i * rows, rows)
        for load in loads[i]:
            load.wait()
        masked = obs[part, :] * sel[part, :].astype(F32).astype(BF16)
        log_shift = dot(masked, resp_ref[...])
        weight[part, :] = base_col[i * rows : (i + 1) * rows] * jnp.exp(0.2 * log_shift)

    var_at = iota((variations, variations // 2), 0)
    mine = iota((variations, variations // 2), 1) == var_at // 2
    pull = jnp.sum(jnp.where(mine, pull_ref[...], 0.0), axis=1, keepdims=True)
    odd = iota((variations, 1), 0) % 2
    coef = jnp.maximum(jnp.where(odd == 0, pull, -pull), 0.0)
    w = weight[...]
    u_all[my_sys] = jnp.sum(coef * (w.T - base), axis=0, keepdims=True)

    pl.semaphore_wait(barrier, n_ev - 1 + n_sys - 1)

    u_copies = []
    for q in range(1, n_sys):
        u_copies.append(pltpu.make_async_remote_copy(
            src_ref=u_all.at[my_sys],
            dst_ref=u_all.at[my_sys],
            send_sem=u_send_sem.at[q],
            recv_sem=u_recv_sem.at[q],
            device_id={"sys": lax.rem(my_sys + q, n_sys)},
            device_id_type=MESH,
        ))
        u_copies[-1].start()

    halves = parts(w, 2)
    chunk = 4
    for i in range(chunk):
        count = n_ev * K // chunk
        pick = onehot(iota((count, events), 0) + i * count == slot)
        send[pl.ds(i * count, count), :] = sum(dot(pick, half) for half in halves)

    def row_copy(d):
        to = lax.rem(me + d, n_ev)
        return pltpu.make_async_remote_copy(
            src_ref=send.at[pl.ds(pl.multiple_of(to * K, 8), K)],
            dst_ref=recv.at[pl.ds(pl.multiple_of(d * K, 8), K)],
            send_sem=send_sem,
            recv_sem=recv_sem,
            device_id={"ev": to},
            device_id_type=MESH,
        )

    def send_rows(i, carry):
        row_copy(lax.rem(i * 27, n_ev)).start()
        return carry

    lax.fori_loop(1, n_ev, send_rows, 0)
    recv[pl.ds(0, K), :] = send[pl.ds(pl.multiple_of(me * K, 8), K), :]

    for copy in u_copies:
        copy.wait()
    u = base
    for q in range(n_sys):
        u = u + u_all[q]
    at_bin = onehot(iota((128, events), 0) == rank)
    at_u = onehot(iota((128, events), 0) - U_LANE == rank)
    row = dot_nt(jnp.where(in_channel, bin_ref[...].astype(F32), 0.0).astype(BF16), at_bin)
    for piece in parts(jnp.where(in_channel, u, 0.0), 3):
        row = row + dot_nt(piece, at_u)
    row = jnp.where(iota(row.shape, 1) >= N_LANE, most, row)
    meta[...] = row[:, None, :]

    def meta_copy(d):
        to = lax.rem(me + d, n_ev)
        return pltpu.make_async_remote_copy(
            src_ref=meta.at[to],
            dst_ref=meta_in.at[d],
            send_sem=meta_send_sem,
            recv_sem=meta_recv_sem,
            device_id={"ev": to},
            device_id_type=MESH,
        )

    def send_meta(i, carry):
        meta_copy(lax.rem(i * 27, n_ev)).start()
        return carry

    lax.fori_loop(1, n_ev, send_meta, 0)
    meta_in[0] = meta[me]

    others = pl.ds(1, n_ev - 1)
    all_meta = pltpu.make_async_remote_copy(
        src_ref=meta.at[others], dst_ref=meta_in.at[others], send_sem=meta_send_sem,
        recv_sem=meta_recv_sem, device_id={"ev": lax.rem(me + 1, n_ev)}, device_id_type=MESH,
    )
    all_meta.wait()
    got = meta_in[:, 0, :]
    most_ref[...] = jnp.max(got[:, N_LANE:], axis=0, keepdims=True)
    slots = n_ev * K
    at = iota((1, slots), 1).astype(F32)
    sender = jnp.floor((at + 0.5) * (1.0 / K))
    place = (at - K * sender).astype(jnp.int32)
    sender = sender.astype(jnp.int32)
    ours = iota((n_ev, slots), 0) == sender
    spread_bin = onehot(iota((128, slots), 0) == place)
    spread_u = onehot(iota((128, slots), 0) - U_LANE == place)
    pieces = parts(got, 3)
    bins = jnp.sum(jnp.where(ours, dot(pieces[0], spread_bin), 0.0), axis=0, keepdims=True)
    terms = sum(dot(piece, spread_u) for piece in pieces)
    terms = jnp.sum(jnp.where(ours, terms, 0.0), axis=0, keepdims=True)
    in_bin = iota((B, slots), 0) == bins.astype(jnp.int32)
    filled = jnp.sum(jnp.where(in_bin, terms, 0.0), axis=1, keepdims=True)
    expected_ref[...] = jnp.broadcast_to(filled, (B, 128)).T[0:1]

    some = pl.ds(K, (n_ev - 1) * K)
    all_rows = pltpu.make_async_remote_copy(
        src_ref=send.at[some], dst_ref=recv.at[some], send_sem=send_sem, recv_sem=recv_sem,
        device_id={"ev": lax.rem(me + 1, n_ev)}, device_id_type=MESH,
    )
    all_rows.wait()
    wide = jnp.concatenate(parts(recv[...], 2), axis=1)
    total = dot(onehot(in_bin), wide)
    hist_ref[...] = (total[:, :variations] + total[:, variations:]).T


def local(n_ev, n_sys, observables, selection, base_weight, category, bin_number, response, nuisance_pulls):
    events, features = observables.shape
    variations = response.shape[1]

    def call(later, *lead):
        vmem = pl.BlockSpec(memory_space=pltpu.VMEM)
        hbm = pl.BlockSpec(memory_space=pl.ANY)
        return pl.pallas_call(
            functools.partial(exchange, n_ev, n_sys, later),
            out_shape=(
                jax.ShapeDtypeStruct((variations, B), F32),
                jax.ShapeDtypeStruct((1, B), F32),
                jax.ShapeDtypeStruct((1, 128 - N_LANE), F32),
            ),
            in_specs=[pl.BlockSpec(memory_space=pltpu.SMEM)] * len(lead) + [hbm] * 2 + [vmem] * 5,
            out_specs=(vmem, vmem, vmem),
            scratch_shapes=[
                pltpu.VMEM((events, features), BF16),
                pltpu.VMEM((events, features), jnp.int32),
                pltpu.VMEM((events, variations), F32),
                pltpu.VMEM((n_ev * K, variations), F32),
                pltpu.VMEM((n_ev * K, variations), F32),
                pltpu.VMEM((n_ev, 1, 128), F32),
                pltpu.VMEM((n_ev, 1, 128), F32),
                pltpu.VMEM((n_sys, 1, events), F32),
                pltpu.SemaphoreType.DMA((2, 4)),
                pltpu.SemaphoreType.DMA((n_sys,)),
                pltpu.SemaphoreType.DMA((n_sys,)),
                pltpu.SemaphoreType.DMA,
                pltpu.SemaphoreType.DMA,
                pltpu.SemaphoreType.DMA,
                pltpu.SemaphoreType.DMA,
            ],
            compiler_params=pltpu.CompilerParams(
                collective_id=1 if later else 0, has_side_effects=True, vmem_limit_bytes=32 << 20
            ),
            name="later_round" if later else "first_round",
        )(
            *lead,
            observables,
            selection,
            base_weight.reshape(1, events),
            category.reshape(1, events),
            bin_number.reshape(1, events),
            response,
            nuisance_pulls.reshape(1, -1),
        )

    templates, expected, most = call(False)
    largest = most[0, 0].astype(jnp.int32)

    def more(carry):
        return carry[0] * K < largest

    def next_round(carry):
        index, templates, expected = carry
        extra, extra_expected, _ = call(True, index.reshape(1))
        return index + 1, templates + extra, expected + extra_expected

    _, templates, expected = lax.while_loop(more, next_round, (jnp.int32(1), templates, expected))
    return templates[None], expected


def solution(mesh):
    placed = (P("ev", None), P("ev", None), P("ev"), P("ev"), P("ev"), P(None, "sys"), P("sys"))
    return jax.shard_map(
        functools.partial(local, mesh.shape["ev"], mesh.shape["sys"]),
        mesh=mesh,
        in_specs=placed,
        out_specs=(P("ev", "sys", None), P("ev", None)),
        check_vma=False,
    )
```

time: 650 us -> 31 us (0.05)
  waiting for transfers between devices: 586 us -> 0 us
  Pallas kernels: 0 us -> 28.2 us
  between operations: 14.8 us -> 0.77 us
  matrix products: 13.8 us -> 0 us
  local copies, waits for them, and re-layouts: 12.9 us -> 1.86 us
  blocking collectives: 10.5 us -> 0 us
  starting transfers between devices: 6.9 us -> 0 us
    unnamed x2 -> x0, waiting for transfers between devices: 578 us -> none
    pallas_call x0 -> x1, Pallas kernels: none -> 28.2 us  [call(): pl.pallas_call(functools.partial(exchange, n_ev, n_sys, later), out_shape...]
    dot_general x3 -> x0, matrix products: 13.8 us -> none  [the longest x2 12.1 us: contract_rows(): lax.dot_general(stacked, onehot, (((0,), (0,)), ((), ())), precision=lax....]
    psum x1 -> x0, blocking collectives: 10.5 us -> none  [local(): change_total = lax.psum(jnp.sum(changes, axis=1), 'sys')]
    reshape x1 -> x0, local copies, waits for them, and re-layouts: 9.41 us -> none  [local(): summed.reshape(kept_rows * lax.axis_size('ev'), C * B)]
    all_to_all x1 -> x0, waiting for transfers between devices: 7.88 us -> none  [local(): lax.all_to_all(received, 'ev', split_axis=1, concat_axis=0, tiled=True)]
    all_to_all x1 -> x0, starting transfers between devices: 6.86 us -> none  [local(): lax.all_to_all(received, 'ev', split_axis=1, concat_axis=0, tiled=True)]
  transfers between devices with their start and end apart: 2 -> 0, of which waited for: 2 -> 0; matrix products, arithmetic and copies ran while one was open for 0% -> 0% of each run, Pallas kernels for 0% -> 0%
where the time goes in v1:
time: 31 us; the launch traced here: 30.8 us
  Pallas kernels  28.2 us (91%)
  local copies, waits for them, and re-layouts  1.86 us (6%)
  between operations  0.77 us (2%)
    pallas_call x1, Pallas kernels, call(): pl.pallas_call(functools.partial(exchange, n_ev, n_sys, later), out_shape...  28.2 us
    unnamed x16, local copies, waits for them, and re-layouts  1.86 us

profile of v1, /device:TPU:1, one launch (start us, length us, event | category | flops | bytes accessed | tf_op | source)
XLA Modules:
  0.0 30.8 jit_solution(5199409752399990096)
XLA Ops:
  0.6 0.0 copy-start
  0.6 0.0 copy-start.1
  0.7 0.0 copy-start.2
  0.7 0.0 copy-start.4
  0.7 0.0 copy-start.5
  0.7 28.2 %first_round.1 = (f32[128,256]{1,0:T(8,128)S(1)}, f32[1,256]{1,0:T(1,128)S(1)}, f32[1,64]{1,0:T(1,128)S(1)}) custom-call(bf16[512,512]{1,0:T(8,128)(2,1)} %refs_0_.1, s32[512,512]{1,0:T(8,128)} %refs_1_.1, f32[1,512]{1,0:T(1,128)} %bitcast.24, s32[1,512]{1,0:T(1,128)} %bitcast.26, s32[1,512]{1,0:T(1,128)} %bitcast.28, bf16[512,128]{1,0:T(8,128)(2,1)} %refs_5_.1, ...), custom_call_target="tpu_custom_call" | custom-call | tf_op jit(solution)/shard_map/first_round/pallas_call | solution.py:226
  28.9 0.0 copy-start.3
  29.0 0.0 copy-start.6
  29.0 0.0 copy-done
  29.0 0.0 copy-done.1
  29.0 0.0 copy-done.2
  29.0 0.0 copy-done.4
  29.0 0.0 copy-done.5
  29.0 0.6 %copy-done.3 = f32[512]{0:T(512)S(1)} copy-done((f32[512]{0:T(512)S(1)}, f32[512]{0:T(512)}, u32[]{:S(2)}) %copy-start.3) | copy-done | bytes 2072
  29.6 0.0 copy-done.6
  29.6 0.7 %copy.20 = f32[1,128,256]{2,1,0:T(8,128)} copy(f32[1,128,256]{2,1,0:T(8,128)S(1)} %bitcast.23) | data formatting | bytes 262144
  30.3 0.6 %copy.21 = f32[1,256]{1,0:T(1,128)} copy(f32[1,256]{1,0:T(1,128)S(1)} %get-tuple-element.204) | data formatting | bytes 2048
  (1 shorter events, 0.0 us)
Async XLA Ops:
  0.6 28.3 %copy-start = (s32[512,512]{1,0:T(8,128)S(1)}, s32[512,512]{1,0:T(8,128)}, u32[]{:S(2)}) copy-start(s32[512,512]{1,0:T(8,128)} %refs_1_.1) | copy-start | bytes 3145732
  0.6 28.3 %copy-start.1 = (bf16[512,512]{1,0:T(8,128)(2,1)S(1)}, bf16[512,512]{1,0:T(8,128)(2,1)}, u32[]{:S(2)}) copy-start(bf16[512,512]{1,0:T(8,128)(2,1)} %refs_0_.1) | copy-start | bytes 1572868
  0.7 28.3 %copy-start.2 = (bf16[512,128]{1,0:T(8,128)(2,1)S(1)}, bf16[512,128]{1,0:T(8,128)(2,1)}, u32[]{:S(2)}) copy-start(bf16[512,128]{1,0:T(8,128)(2,1)} %refs_5_.1) | copy-start | bytes 393220
  0.7 28.3 %copy-start.4 = (s32[512]{0:T(512)S(1)}, s32[512]{0:T(512)}, u32[]{:S(2)}) copy-start(s32[512]{0:T(512)} %param.12) | copy-start | bytes 6148
  0.7 28.3 %copy-start.5 = (s32[512]{0:T(512)S(1)}, s32[512]{0:T(512)}, u32[]{:S(2)}) copy-start(s32[512]{0:T(512)} %param.13) | copy-start | bytes 6148
  28.9 0.7 %copy-start.3 = (f32[512]{0:T(512)S(1)}, f32[512]{0:T(512)}, u32[]{:S(2)}) copy-start(f32[512]{0:T(512)} %param.11) | copy-start | bytes 6148
  29.0 0.7 %copy-start.6 = (f32[64]{0:T(128)S(1)}, f32[64]{0:T(128)}, u32[]{:S(2)}) copy-start(f32[64]{0:T(128)} %param.15) | copy-start | bytes 772

commit v2 on v0

v2 whole, which is shorter than its diff:
```python
import functools

import jax
import jax.numpy as jnp
from jax import lax
from jax.experimental import pallas as pl
from jax.experimental.pallas import tpu as pltpu
from jax.sharding import PartitionSpec as P

B = 256
K = 24
STRIDE = 27
PACKS = 8
ARRIVALS = 4
FIRST_PACKS = 6
STEPS = 4
U_LANE = 32
N_LANE = 64
VMEM_BYTES = 48 << 20
MESH = pl.DeviceIdType.MESH
F32 = jnp.float32
BF16 = jnp.bfloat16


def iota(shape, dim):
    return lax.broadcasted_iota(jnp.int32, shape, dim)


def onehot(mask):
    return jnp.where(mask, 1.0, 0.0).astype(BF16)


def parts(x, count):
    out = []
    for _ in range(count):
        piece = x.astype(BF16)
        out.append(piece)
        x = x - piece.astype(F32)
    return out


def dot(a, b):
    return jnp.dot(a, b, preferred_element_type=F32)


def dot_nt(a, b):
    return lax.dot_general(a, b, (((1,), (1,)), ((), ())), preferred_element_type=F32)


def prepare(n_ev, me, hbm_refs, weight, info, vmem_refs, small_sem, load_sem, greet):
    obs_hbm, sel_hbm, base_hbm, cat_hbm, bin_hbm, resp_hbm = hbm_refs
    obs, sel, base_ref, cat_ref, bin_ref, resp_ref = vmem_refs
    events = obs.shape[0]
    variations = weight.shape[1]
    rows = events // STEPS

    small = []
    for i, (source, target) in enumerate((
        (cat_hbm, cat_ref), (bin_hbm, bin_ref), (base_hbm, base_ref), (resp_hbm, resp_ref),
    )):
        small.append(pltpu.make_async_copy(source, target, small_sem.at[i]))
        small[-1].start()
    loads = []
    for i in range(STEPS):
        part = pl.ds(i * rows, rows)
        loads.append((
            pltpu.make_async_copy(obs_hbm.at[part], obs.at[part], load_sem.at[0, i]),
            pltpu.make_async_copy(sel_hbm.at[part], sel.at[part], load_sem.at[1, i]),
        ))
        for load in loads[-1]:
            load.start()
    greet()

    before = onehot(iota((events, events), 0) < iota((events, events), 1))
    for copy in small:
        copy.wait()
    cat = cat_ref[...]
    away = jnp.where(cat < me, cat - me + n_ev, cat - me)
    block = away * pow(STRIDE, -1, n_ev) % n_ev
    in_block = iota((n_ev, events), 0) == block
    ahead = dot(onehot(in_block), before)
    rank = jnp.sum(jnp.where(in_block, ahead, 0.0), axis=0, keepdims=True)
    base = base_ref[...]
    info[0:1, :] = block.astype(F32)
    info[1:2, :] = rank
    info[2:3, :] = bin_ref[...].astype(F32)
    info[3:4, :] = base
    base_col = jnp.broadcast_to(base, (variations, events)).T

    for i in range(STEPS):
        part = pl.ds(i * rows, rows)
        for load in loads[i]:
            load.wait()
        masked = obs[part, :] * sel[part, :].astype(F32).astype(BF16)
        log_shift = dot(masked, resp_ref[...])
        weight[part, :] = base_col[i * rows : (i + 1) * rows] * jnp.exp(0.2 * log_shift)


def exchange(n_ev, n_sys, later, *refs):
    if later:
        (
            round_ref, weight, info, hist_ref, expected_ref,
            send, recv, meta, meta_in, picked, send_sem, recv_sem, meta_send_sem, meta_recv_sem,
        ) = refs
    else:
        hbm_refs, refs = refs[:6], refs[6:]
        (
            pull_hbm, hist_ref, expected_ref, most_ref, weight, info,
            send, recv, meta, meta_in, picked, send_sem, recv_sem, meta_send_sem, meta_recv_sem,
            share, pull_ref, small_sem, share_send_sem, share_recv_sem, *vmem_refs, load_sem,
        ) = refs
    events, variations = weight.shape
    slots = n_ev * K
    me, my_sys = lax.axis_index("ev"), lax.axis_index("sys")
    barrier = pltpu.get_barrier_semaphore()

    half = n_sys // 2
    first_half = my_sys < half

    def greet():
        def signal(d, carry):
            pl.semaphore_signal(
                barrier, inc=1, device_id={"ev": lax.rem(me + d, n_ev)}, device_id_type=MESH
            )
            return carry

        lax.fori_loop(1, n_ev, signal, 0, unroll=7 if n_ev == 64 else 1)
        if later:
            return
        for q in range(n_sys):
            @pl.when(jnp.logical_and(q != my_sys, jnp.logical_or(first_half, q >= half)))
            def _():
                pl.semaphore_signal(barrier, inc=1, device_id={"sys": q}, device_id_type=MESH)

    def share_copy(sender, target):
        return pltpu.make_async_remote_copy(
            src_ref=share.at[my_sys],
            dst_ref=share.at[my_sys],
            send_sem=share_send_sem.at[target],
            recv_sem=share_recv_sem.at[sender],
            device_id={"sys": target},
            device_id_type=MESH,
        )

    if later:
        greet()
        pl.semaphore_wait(barrier, n_ev - 1)
    else:
        pull_copy = pltpu.make_async_copy(pull_hbm, pull_ref, small_sem.at[4])
        pull_copy.start()
        prepare(n_ev, me, hbm_refs, weight, info, vmem_refs, small_sem, load_sem, greet)

        pull_copy.wait()
        var_at = iota((variations, variations // 2), 0)
        mine = iota((variations, variations // 2), 1) == var_at // 2
        pull = jnp.sum(jnp.where(mine, pull_ref[...], 0.0), axis=1, keepdims=True)
        odd = iota((variations, 1), 0) % 2
        coef = jnp.maximum(jnp.where(odd == 0, pull, -pull), 0.0)
        share[my_sys] = jnp.sum(coef * (weight[...].T - info[3:4, :]), axis=0, keepdims=True)
        pl.semaphore_wait(barrier, n_ev - 1 + jnp.where(first_half, half - 1, n_sys - 1))
        for q in range(n_sys):
            @pl.when(jnp.logical_and(q != my_sys, jnp.logical_or(my_sys >= half, q < half)))
            def _():
                share_copy(my_sys, q).start()

    block = info[0:1, :].astype(jnp.int32)
    rank_f = info[1:2, :]
    most = jnp.max(rank_f, axis=1, keepdims=True) + 1.0
    rank = rank_f.astype(jnp.int32)
    if later:
        rank = rank - round_ref[0] * K
    kept = jnp.logical_and(rank >= 0, rank < K)
    slot = jnp.where(kept, block * K + rank, -1)
    rank = jnp.where(kept, rank, -1)

    def to(i):
        return {"ev": lax.rem(me + STRIDE * i % n_ev, n_ev)}

    w = weight[...]
    halves = jnp.concatenate(parts(w, 2), axis=1)
    count = slots // PACKS
    blocks = n_ev // PACKS

    def pack(p):
        pick = onehot(iota((count, events), 0) + p * count == slot)
        both = dot(pick, halves)
        send[pl.ds(p * count, count), :] = both[:, :variations] + both[:, variations:]
        for i in range(p * blocks, (p + 1) * blocks):
            if i > 0:
                pltpu.make_async_remote_copy(
                    src_ref=send.at[pl.ds(i * K, K)],
                    dst_ref=recv.at[pl.ds(i * K, K)],
                    send_sem=send_sem,
                    recv_sem=recv_sem.at[i * ARRIVALS // n_ev],
                    device_id=to(i),
                    device_id_type=MESH,
                ).start()

    for p in range(FIRST_PACKS):
        pack(p)

    if not later:
        @pl.when(first_half)
        def _():
            for q in range(half, n_sys):
                share_copy(q, q).wait_recv()
                share_copy(my_sys, q).start()

        for q in range(n_sys):
            @pl.when(jnp.logical_and(q != my_sys, jnp.logical_or(my_sys >= half, q < half)))
            def _():
                share_copy(q, q).wait_recv()

        term = info[3:4, :]
        for q in range(n_sys):
            term = term + share[q]
        info[3:4, :] = term
    term = info[3:4, :]
    in_block = iota((n_ev, events), 0) == block
    at_bin = onehot(iota((128, events), 0) == rank)
    at_term = onehot(iota((128, events), 0) - U_LANE == rank)
    row = dot_nt(jnp.where(in_block, info[2:3, :], 0.0).astype(BF16), at_bin)
    for piece in parts(jnp.where(in_block, term, 0.0), 3):
        row = row + dot_nt(piece, at_term)
    row = jnp.where(iota(row.shape, 1) >= N_LANE, most, row)
    meta[...] = row[:, None, :]
    for i in range(1, n_ev):
        pltpu.make_async_remote_copy(
            src_ref=meta.at[i], dst_ref=meta_in.at[i], send_sem=meta_send_sem,
            recv_sem=meta_recv_sem, device_id=to(i), device_id_type=MESH,
        ).start()
    meta_in[0] = meta[0]

    for p in range(FIRST_PACKS, PACKS):
        pack(p)
    recv[pl.ds(0, K), :] = send[pl.ds(0, K), :]

    at = iota((1, slots), 1).astype(F32)
    sender = jnp.floor((at + 0.5) * (1.0 / K))
    place = (at - K * sender).astype(jnp.int32)
    ours = iota((n_ev, slots), 0) == sender.astype(jnp.int32)
    spread_bin = onehot(iota((128, slots), 0) == place)
    spread_term = onehot(iota((128, slots), 0) - U_LANE == place)

    others = pl.ds(1, n_ev - 1)
    pltpu.make_async_remote_copy(
        src_ref=meta.at[others], dst_ref=meta_in.at[others], send_sem=meta_send_sem,
        recv_sem=meta_recv_sem, device_id=to(1), device_id_type=MESH,
    ).wait()
    got = meta_in[:, 0, :]
    if not later:
        most_ref[...] = jnp.max(got[:, N_LANE:], axis=0, keepdims=True)
    pieces = parts(got, 3)
    bins = jnp.sum(jnp.where(ours, dot(pieces[0], spread_bin), 0.0), axis=0, keepdims=True)
    terms = sum(dot(piece, spread_term) for piece in pieces)
    terms = jnp.sum(jnp.where(ours, terms, 0.0), axis=0, keepdims=True)
    in_bin = iota((B, slots), 0) == bins.astype(jnp.int32)
    filled = jnp.sum(jnp.where(in_bin, terms, 0.0), axis=1, keepdims=True)
    expected_ref[...] = jnp.broadcast_to(filled, (B, 128)).T[0:1]
    picked[...] = onehot(in_bin)

    def arrive(a):
        first = max(a * n_ev // ARRIVALS, 1)
        some = pl.ds(first * K, ((a + 1) * n_ev // ARRIVALS - first) * K)
        pltpu.make_async_remote_copy(
            src_ref=send.at[some], dst_ref=recv.at[some], send_sem=send_sem,
            recv_sem=recv_sem.at[a], device_id=to(1), device_id_type=MESH,
        ).wait_recv()

    def filled_by(first, last):
        wide = jnp.concatenate(parts(recv[first:last, :], 2), axis=1)
        return dot(picked[:, first:last], wide)

    early = slots // ARRIVALS * (ARRIVALS - 1)
    for a in range(ARRIVALS - 1):
        arrive(a)
    total = filled_by(0, early)
    arrive(ARRIVALS - 1)
    total = total + filled_by(early, slots)
    hist_ref[...] = (total[:, :variations] + total[:, variations:]).T

    sent = pl.ds(K, slots - K)
    pltpu.make_async_remote_copy(
        src_ref=send.at[sent], dst_ref=recv.at[sent], send_sem=send_sem,
        recv_sem=recv_sem.at[0], device_id=to(1), device_id_type=MESH,
    ).wait_send()
    if not later:
        for q in range(n_sys):
            @pl.when(q != my_sys)
            def _():
                share_copy(my_sys, q).wait_send()


def in_hbm(x):
    return pltpu.with_memory_space_constraint(x, pltpu.HBM)


def store(hist_ref, expected_ref, templates_hbm, expected_hbm, sem):
    copies = (
        pltpu.make_async_copy(hist_ref, templates_hbm.at[0], sem.at[0]),
        pltpu.make_async_copy(expected_ref, expected_hbm, sem.at[1]),
    )
    for copy in copies:
        copy.start()
    for copy in copies:
        copy.wait()


def finish(templates, expected):
    vmem = pl.BlockSpec(memory_space=pltpu.VMEM)
    hbm = pl.BlockSpec(memory_space=pltpu.HBM)
    return pl.pallas_call(
        store,
        out_shape=(
            jax.ShapeDtypeStruct((1,) + templates.shape, F32),
            jax.ShapeDtypeStruct(expected.shape, F32),
        ),
        in_specs=[vmem] * 2,
        out_specs=(hbm, hbm),
        scratch_shapes=[pltpu.SemaphoreType.DMA((2,))],
        name="store",
    )(templates, expected)


def local(n_ev, n_sys, observables, selection, base_weight, category, bin_number, response, nuisance_pulls):
    events, features = observables.shape
    variations = response.shape[1]
    vmem = pl.BlockSpec(memory_space=pltpu.VMEM)
    hbm = pl.BlockSpec(memory_space=pltpu.HBM)
    slots = n_ev * K
    results = (
        jax.ShapeDtypeStruct((variations, B), F32),
        jax.ShapeDtypeStruct((1, B), F32),
    )
    scratch = [
        pltpu.VMEM((slots, variations), F32),
        pltpu.VMEM((slots, variations), F32),
        pltpu.VMEM((n_ev, 1, 128), F32),
        pltpu.VMEM((n_ev, 1, 128), F32),
        pltpu.VMEM((B, slots), BF16),
        pltpu.SemaphoreType.DMA,
        pltpu.SemaphoreType.DMA((ARRIVALS,)),
        pltpu.SemaphoreType.DMA,
        pltpu.SemaphoreType.DMA,
    ]
    templates, expected, most, weight, info = pl.pallas_call(
        functools.partial(exchange, n_ev, n_sys, False),
        out_shape=results + (
            jax.ShapeDtypeStruct((1, 128 - N_LANE), F32),
            jax.ShapeDtypeStruct((events, variations), F32),
            jax.ShapeDtypeStruct((8, events), F32),
        ),
        in_specs=[hbm] * 7,
        out_specs=(vmem,) * 5,
        scratch_shapes=scratch + [
            pltpu.VMEM((n_sys, 1, events), F32),
            pltpu.VMEM((1, variations // 2), F32),
            pltpu.SemaphoreType.DMA((5,)),
            pltpu.SemaphoreType.DMA((n_sys,)),
            pltpu.SemaphoreType.DMA((n_sys,)),
            pltpu.VMEM((events, features), BF16),
            pltpu.VMEM((events, features), jnp.int32),
            pltpu.VMEM((1, events), F32),
            pltpu.VMEM((1, events), jnp.int32),
            pltpu.VMEM((1, events), jnp.int32),
            pltpu.VMEM((features, variations), BF16),
            pltpu.SemaphoreType.DMA((2, STEPS)),
        ],
        compiler_params=pltpu.CompilerParams(
            collective_id=0, has_side_effects=True, vmem_limit_bytes=VMEM_BYTES
        ),
        name="first_round",
    )(
        in_hbm(observables),
        in_hbm(selection),
        in_hbm(base_weight.reshape(1, events)),
        in_hbm(category.reshape(1, events)),
        in_hbm(bin_number.reshape(1, events)),
        in_hbm(response),
        in_hbm(nuisance_pulls.reshape(1, -1)),
    )
    largest = most[0, 0].astype(jnp.int32)

    def more(carry):
        return carry[0] * K < largest

    def next_round(carry):
        index, templates, expected = carry
        extra, extra_expected = pl.pallas_call(
            functools.partial(exchange, n_ev, n_sys, True),
            out_shape=results,
            in_specs=[pl.BlockSpec(memory_space=pltpu.SMEM), vmem, vmem],
            out_specs=(vmem, vmem),
            scratch_shapes=scratch,
            compiler_params=pltpu.CompilerParams(
                collective_id=1, has_side_effects=True, vmem_limit_bytes=VMEM_BYTES
            ),
            name="later_round",
        )(index.reshape(1), weight, info)
        return index + 1, templates + extra, expected + extra_expected

    _, templates, expected = lax.while_loop(more, next_round, (jnp.int32(1), templates, expected))
    return finish(templates, expected)


def solution(mesh):
    placed = (P("ev", None), P("ev", None), P("ev"), P("ev"), P("ev"), P(None, "sys"), P("sys"))
    return jax.shard_map(
        functools.partial(local, mesh.shape["ev"], mesh.shape["sys"]),
        mesh=mesh,
        in_specs=placed,
        out_specs=(P("ev", "sys", None), P("ev", None)),
        check_vma=False,
    )
```

time: 650 us -> 24.6 us (0.04)
  waiting for transfers between devices: 586 us -> 0 us
  Pallas kernels: 0 us -> 23.8 us
  between operations: 14.8 us -> 0.68 us
  matrix products: 13.8 us -> 0 us
  local copies, waits for them, and re-layouts: 12.9 us -> 0 us
  blocking collectives: 10.5 us -> 0 us
  starting transfers between devices: 6.9 us -> 0 us
    unnamed x2 -> x0, waiting for transfers between devices: 578 us -> none
    pallas_call x0 -> x2, Pallas kernels: none -> 23.8 us  [the longest x1 23.1 us: local(): pl.pallas_call(functools.partial(exchange, n_ev, n_sys, False), out_shape...]
    dot_general x3 -> x0, matrix products: 13.8 us -> none  [the longest x2 12.1 us: contract_rows(): lax.dot_general(stacked, onehot, (((0,), (0,)), ((), ())), precision=lax....]
    psum x1 -> x0, blocking collectives: 10.5 us -> none  [local(): change_total = lax.psum(jnp.sum(changes, axis=1), 'sys')]
    reshape x1 -> x0, local copies, waits for them, and re-layouts: 9.41 us -> none  [local(): summed.reshape(kept_rows * lax.axis_size('ev'), C * B)]
    all_to_all x1 -> x0, waiting for transfers between devices: 7.88 us -> none  [local(): lax.all_to_all(received, 'ev', split_axis=1, concat_axis=0, tiled=True)]
    all_to_all x1 -> x0, starting transfers between devices: 6.86 us -> none  [local(): lax.all_to_all(received, 'ev', split_axis=1, concat_axis=0, tiled=True)]
  transfers between devices with their start and end apart: 2 -> 0, of which waited for: 2 -> 0; matrix products, arithmetic and copies ran while one was open for 0% -> 0% of each run, Pallas kernels for 0% -> 0%
where the time goes in v2:
time: 24.6 us; the launch traced here: 24.5 us
  Pallas kernels  23.8 us (97%)
  between operations  0.68 us (3%)
    pallas_call x1, Pallas kernels, local(): pl.pallas_call(functools.partial(exchange, n_ev, n_sys, False), out_shape...  23.1 us
    pallas_call x1, Pallas kernels, finish(): pl.pallas_call(store, out_shape=(jax.ShapeDtypeStruct((1,) + templates.sh...  0.68 us

profile of v2, /device:TPU:1, one launch (start us, length us, event | category | flops | bytes accessed | tf_op | source)
XLA Modules:
  0.0 24.5 jit_solution(1082031440972110662)
XLA Ops:
  0.6 23.1 %first_round.1 = (f32[128,256]{1,0:T(8,128)S(1)}, f32[1,256]{1,0:T(1,128)S(1)}, f32[1,64]{1,0:T(1,128)S(1)}, f32[512,128]{1,0:T(8,128)S(1)}, f32[8,512]{1,0:T(8,128)S(1)}) custom-call(bf16[512,512]{1,0:T(8,128)(2,1)} %refs_0_.1, s32[512,512]{1,0:T(8,128)} %refs_1_.1, f32[1,512]{1,0:T(1,128)} %bitcast.10, s32[1,512]{1,0:T(1,128)} %bitcast.11, ...), custom_call_target="tpu_custom_call" | custom-call | tf_op jit(solution)/shard_map/first_round/pallas_call | solution.py:346
  23.8 0.7 %store.1 = (f32[1,128,256]{2,1,0:T(8,128)}, f32[1,256]{1,0:T(1,128)}) custom-call(f32[128,256]{1,0:T(8,128)S(1)} %get-tuple-element.48.hist_ref, f32[1,256]{1,0:T(1,128)S(1)} %get-tuple-element.49.expected_ref), custom_call_target="tpu_custom_call" | custom-call | tf_op jit(solution)/shard_map/store/pallas_call | solution.py:312
  (1 shorter events, 0.0 us)

commit v3 on v2

--- a/solution.py
+++ b/solution.py
@@ -9,13 +9,14 @@
 
 B = 256
 K = 24
+PITCH = 32
+SECOND_LANE = 32
+N_LANE = 64
 STRIDE = 27
 PACKS = 8
+FIRST_PACKS = 8
 ARRIVALS = 4
-FIRST_PACKS = 6
 STEPS = 4
-U_LANE = 32
-N_LANE = 64
 VMEM_BYTES = 48 << 20
 MESH = pl.DeviceIdType.MESH
 F32 = jnp.float32
@@ -45,6 +46,12 @@
 
 def dot_nt(a, b):
     return lax.dot_general(a, b, (((1,), (1,)), ((), ())), preferred_element_type=F32)
+
+
+def far(i):
+    away = STRIDE * i % 64
+    x, z, y = away // 2 % 4, away // 8 % 2, away // 16
+    return -(min(x, 4 - x) + z + min(y, 4 - y))
 
 
 def prepare(n_ev, me, hbm_refs, weight, info, vmem_refs, small_sem, load_sem, greet):
@@ -100,37 +107,43 @@
     if later:
         (
             round_ref, weight, info, hist_ref, expected_ref,
-            send, recv, meta, meta_in, picked, send_sem, recv_sem, meta_send_sem, meta_recv_sem,
+            send, recv, terms, terms_in, picked, morph,
+            send_sem, recv_sem, terms_send_sem, terms_recv_sem, morph_send_sem, morph_recv_sem,
         ) = refs
     else:
         hbm_refs, refs = refs[:6], refs[6:]
         (
             pull_hbm, hist_ref, expected_ref, most_ref, weight, info,
-            send, recv, meta, meta_in, picked, send_sem, recv_sem, meta_send_sem, meta_recv_sem,
+            send, recv, terms, terms_in, picked, morph,
+            send_sem, recv_sem, terms_send_sem, terms_recv_sem, morph_send_sem, morph_recv_sem,
             share, pull_ref, small_sem, share_send_sem, share_recv_sem, *vmem_refs, load_sem,
         ) = refs
     events, variations = weight.shape
-    slots = n_ev * K
+    slots = n_ev * PITCH
     me, my_sys = lax.axis_index("ev"), lax.axis_index("sys")
     barrier = pltpu.get_barrier_semaphore()
 
     half = n_sys // 2
     first_half = my_sys < half
+    partner = n_sys - 1 - my_sys
+
+    def to(i):
+        peer = me + STRIDE * i % n_ev
+        return {"ev": jnp.where(peer >= n_ev, peer - n_ev, peer)}
 
     def greet():
-        def signal(d, carry):
-            pl.semaphore_signal(
-                barrier, inc=1, device_id={"ev": lax.rem(me + d, n_ev)}, device_id_type=MESH
-            )
-            return carry
-
-        lax.fori_loop(1, n_ev, signal, 0, unroll=7 if n_ev == 64 else 1)
         if later:
-            return
-        for q in range(n_sys):
-            @pl.when(jnp.logical_and(q != my_sys, jnp.logical_or(first_half, q >= half)))
+            @pl.when(my_sys >= half)
             def _():
-                pl.semaphore_signal(barrier, inc=1, device_id={"sys": q}, device_id_type=MESH)
+                pl.semaphore_signal(barrier, inc=1, device_id={"sys": partner}, device_id_type=MESH)
+        else:
+            for q in range(n_sys):
+                @pl.when(jnp.logical_and(q != my_sys, jnp.logical_or(first_half, q >= half)))
+                def _():
+                    pl.semaphore_signal(barrier, inc=1, device_id={"sys": q}, device_id_type=MESH)
+
+        for i in sorted(range(1, n_ev), key=far):
+            pl.semaphore_signal(barrier, inc=1, device_id=to(i), device_id_type=MESH)
 
     def share_copy(sender, target):
         return pltpu.make_async_remote_copy(
@@ -142,12 +155,17 @@
             device_id_type=MESH,
         )
 
+    recv[:, K:, :] = jnp.zeros((n_ev, PITCH - K, variations), F32)
     if later:
         greet()
-        pl.semaphore_wait(barrier, n_ev - 1)
+        pl.semaphore_wait(barrier, n_ev - 1 + jnp.where(first_half, 1, 0))
     else:
         pull_copy = pltpu.make_async_copy(pull_hbm, pull_ref, small_sem.at[4])
         pull_copy.start()
+        @pl.when(my_sys >= half)
+        def _():
+            share[0:half] = jnp.zeros((half, 1, events), F32)
+
         prepare(n_ev, me, hbm_refs, weight, info, vmem_refs, small_sem, load_sem, greet)
 
         pull_copy.wait()
@@ -170,26 +188,28 @@
     if later:
         rank = rank - round_ref[0] * K
     kept = jnp.logical_and(rank >= 0, rank < K)
-    slot = jnp.where(kept, block * K + rank, -1)
+    slot = jnp.where(kept, block * PITCH + rank, -1)
     rank = jnp.where(kept, rank, -1)
-
-    def to(i):
-        return {"ev": lax.rem(me + STRIDE * i % n_ev, n_ev)}
-
-    w = weight[...]
-    halves = jnp.concatenate(parts(w, 2), axis=1)
-    count = slots // PACKS
+    in_block = iota((n_ev, events), 0) == block
+    at_place = onehot(iota((128, events), 0) == rank)
+    tags = dot_nt(jnp.where(in_block, info[2:3, :], 0.0).astype(BF16), at_place)
+    tags = jnp.where(iota(tags.shape, 1) >= N_LANE, most, tags)
+
+    halves = jnp.concatenate(parts(weight[...], 2), axis=1)
     blocks = n_ev // PACKS
+    count = blocks * PITCH
 
     def pack(p):
         pick = onehot(iota((count, events), 0) + p * count == slot)
         both = dot(pick, halves)
-        send[pl.ds(p * count, count), :] = both[:, :variations] + both[:, variations:]
+        both = (both[:, :variations] + both[:, variations:]).reshape(blocks, PITCH, variations)
+        tag = tags[p * blocks : (p + 1) * blocks, None, :]
+        send[pl.ds(p * blocks, blocks)] = jnp.where(iota(both.shape, 1) == K, tag, both)
         for i in range(p * blocks, (p + 1) * blocks):
             if i > 0:
                 pltpu.make_async_remote_copy(
-                    src_ref=send.at[pl.ds(i * K, K)],
-                    dst_ref=recv.at[pl.ds(i * K, K)],
+                    src_ref=send.at[i, pl.ds(0, K + 1)],
+                    dst_ref=recv.at[i, pl.ds(0, K + 1)],
                     send_sem=send_sem,
                     recv_sem=recv_sem.at[i * ARRIVALS // n_ev],
                     device_id=to(i),
@@ -198,95 +218,108 @@
 
     for p in range(FIRST_PACKS):
         pack(p)
+    recv[0, :, :] = send[0, :, :]
 
     if not later:
-        @pl.when(first_half)
-        def _():
-            for q in range(half, n_sys):
+        for q in range(n_sys):
+            @pl.when(jnp.logical_and(q != my_sys, jnp.logical_or(first_half, q >= half)))
+            def _():
                 share_copy(q, q).wait_recv()
-                share_copy(my_sys, q).start()
-
+
+        info[3:4, :] = info[3:4, :] + sum(share[q] for q in range(1, half)) + share[0]
+        info[4:5, :] = sum(share[q] for q in range(half + 1, n_sys)) + share[half]
+    pieces = parts(info[3:4, :], 2) + parts(info[4:5, :], 2)
+    stacked = [jnp.where(in_block, piece.astype(F32), 0.0).astype(BF16) for piece in pieces]
+    row = dot_nt(jnp.concatenate(stacked, axis=0), at_place)
+    row = (
+        row[:n_ev] + row[n_ev : 2 * n_ev]
+        + pltpu.roll(row[2 * n_ev : 3 * n_ev] + row[3 * n_ev :], SECOND_LANE, axis=1)
+    )
+    terms[...] = row[:, None, :]
+
+    def terms_copy(blocks, peer):
+        return pltpu.make_async_remote_copy(
+            src_ref=terms.at[blocks], dst_ref=terms_in.at[blocks], send_sem=terms_send_sem,
+            recv_sem=terms_recv_sem, device_id=to(peer), device_id_type=MESH,
+        )
+
+    for i in range(1, n_ev):
+        terms_copy(i, i).start()
+    terms_in[0] = terms[0]
+    for p in range(FIRST_PACKS, PACKS):
+        pack(p)
+
+    blocks = n_ev // ARRIVALS
+    count = blocks * PITCH
+    at = iota((1, count), 1)
+    place = at % PITCH
+    used = place < K
+    ours = iota((blocks, count), 0) == at // PITCH
+    spread = onehot(jnp.logical_and(iota((128, count), 0) == place, used))
+
+    def flat(rows):
+        spaced = dot(rows, spread).reshape(-1, blocks, count)
+        return jnp.sum(jnp.where(ours[None], spaced, 0.0), axis=1)
+
+    def arrived(a):
+        first = a * blocks
+        some = pl.ds(max(first, 1), first + blocks - max(first, 1))
+        pltpu.make_async_remote_copy(
+            src_ref=send.at[some, pl.ds(0, K + 1)], dst_ref=recv.at[some, pl.ds(0, K + 1)],
+            send_sem=send_sem, recv_sem=recv_sem.at[a], device_id=to(1), device_id_type=MESH,
+        ).wait_recv()
+        tag = recv[pl.ds(first, blocks), K, :]
+        bins = jnp.where(used, flat(tag.astype(BF16)), -1.0).astype(jnp.int32)
+        in_bin = onehot(iota((B, count), 0) == bins)
+        picked[:, a * count : (a + 1) * count] = in_bin
+        rows = recv[pl.ds(first, blocks)].reshape(count, variations)
+        return dot(in_bin, jnp.concatenate(parts(rows, 2), axis=1)), jnp.max(tag[:, N_LANE:], axis=0, keepdims=True)
+
+    total, most = arrived(0)
+    for a in range(1, ARRIVALS):
+        more_total, more_most = arrived(a)
+        total, most = total + more_total, jnp.maximum(most, more_most)
+    hist_ref[...] = (total[:, :variations] + total[:, variations:]).T
+    if not later:
+        most_ref[...] = most
+
+    terms_copy(pl.ds(1, n_ev - 1), 1).wait()
+    got = terms_in[:, 0, :]
+    pieces = parts(got, 2) + parts(pltpu.roll(got, 128 - SECOND_LANE, axis=1), 2)
+    lanes = [
+        flat(jnp.concatenate([piece[a * blocks : (a + 1) * blocks] for piece in pieces], axis=0))
+        for a in range(ARRIVALS)
+    ]
+    lanes = jnp.concatenate([jnp.concatenate(lanes, axis=1), jnp.zeros((4, slots), F32)], axis=0)
+    morphed = dot_nt(lanes.astype(BF16), picked[...])
+    morph_copy = pltpu.make_async_remote_copy(
+        src_ref=morph, dst_ref=morph, send_sem=morph_send_sem, recv_sem=morph_recv_sem,
+        device_id={"sys": partner}, device_id_type=MESH,
+    )
+
+    @pl.when(first_half)
+    def _():
+        morph[...] = morphed[0:1] + morphed[1:2]
+        morph_copy.start()
+
+    @pl.when(my_sys >= half)
+    def _():
+        morph_copy.wait_recv()
+
+    expected_ref[...] = morph[...] + (morphed[2:3] + morphed[3:4])
+
+    sent = pl.ds(1, n_ev - 1)
+    pltpu.make_async_remote_copy(
+        src_ref=send.at[sent, pl.ds(0, K + 1)], dst_ref=recv.at[sent, pl.ds(0, K + 1)],
+        send_sem=send_sem, recv_sem=recv_sem.at[0], device_id=to(1), device_id_type=MESH,
+    ).wait_send()
+    @pl.when(first_half)
+    def _():
+        morph_copy.wait_send()
+
+    if not later:
         for q in range(n_sys):
             @pl.when(jnp.logical_and(q != my_sys, jnp.logical_or(my_sys >= half, q < half)))
-            def _():
-                share_copy(q, q).wait_recv()
-
-        term = info[3:4, :]
-        for q in range(n_sys):
-            term = term + share[q]
-        info[3:4, :] = term
-    term = info[3:4, :]
-    in_block = iota((n_ev, events), 0) == block
-    at_bin = onehot(iota((128, events), 0) == rank)
-    at_term = onehot(iota((128, events), 0) - U_LANE == rank)
-    row = dot_nt(jnp.where(in_block, info[2:3, :], 0.0).astype(BF16), at_bin)
-    for piece in parts(jnp.where(in_block, term, 0.0), 3):
-        row = row + dot_nt(piece, at_term)
-    row = jnp.where(iota(row.shape, 1) >= N_LANE, most, row)
-    meta[...] = row[:, None, :]
-    for i in range(1, n_ev):
-        pltpu.make_async_remote_copy(
-            src_ref=meta.at[i], dst_ref=meta_in.at[i], send_sem=meta_send_sem,
-            recv_sem=meta_recv_sem, device_id=to(i), device_id_type=MESH,
-        ).start()
-    meta_in[0] = meta[0]
-
-    for p in range(FIRST_PACKS, PACKS):
-        pack(p)
-    recv[pl.ds(0, K), :] = send[pl.ds(0, K), :]
-
-    at = iota((1, slots), 1).astype(F32)
-    sender = jnp.floor((at + 0.5) * (1.0 / K))
-    place = (at - K * sender).astype(jnp.int32)
-    ours = iota((n_ev, slots), 0) == sender.astype(jnp.int32)
-    spread_bin = onehot(iota((128, slots), 0) == place)
-    spread_term = onehot(iota((128, slots), 0) - U_LANE == place)
-
-    others = pl.ds(1, n_ev - 1)
-    pltpu.make_async_remote_copy(
-        src_ref=meta.at[others], dst_ref=meta_in.at[others], send_sem=meta_send_sem,
-        recv_sem=meta_recv_sem, device_id=to(1), device_id_type=MESH,
-    ).wait()
-    got = meta_in[:, 0, :]
-    if not later:
-        most_ref[...] = jnp.max(got[:, N_LANE:], axis=0, keepdims=True)
-    pieces = parts(got, 3)
-    bins = jnp.sum(jnp.where(ours, dot(pieces[0], spread_bin), 0.0), axis=0, keepdims=True)
-    terms = sum(dot(piece, spread_term) for piece in pieces)
-    terms = jnp.sum(jnp.where(ours, terms, 0.0), axis=0, keepdims=True)
-    in_bin = iota((B, slots), 0) == bins.astype(jnp.int32)
-    filled = jnp.sum(jnp.where(in_bin, terms, 0.0), axis=1, keepdims=True)
-    expected_ref[...] = jnp.broadcast_to(filled, (B, 128)).T[0:1]
-    picked[...] = onehot(in_bin)
-
-    def arrive(a):
-        first = max(a * n_ev // ARRIVALS, 1)
-        some = pl.ds(first * K, ((a + 1) * n_ev // ARRIVALS - first) * K)
-        pltpu.make_async_remote_copy(
-            src_ref=send.at[some], dst_ref=recv.at[some], send_sem=send_sem,
-            recv_sem=recv_sem.at[a], device_id=to(1), device_id_type=MESH,
-        ).wait_recv()
-
-    def filled_by(first, last):
-        wide = jnp.concatenate(parts(recv[first:last, :], 2), axis=1)
-        return dot(picked[:, first:last], wide)
-
-    early = slots // ARRIVALS * (ARRIVALS - 1)
-    for a in range(ARRIVALS - 1):
-        arrive(a)
-    total = filled_by(0, early)
-    arrive(ARRIVALS - 1)
-    total = total + filled_by(early, slots)
-    hist_ref[...] = (total[:, :variations] + total[:, variations:]).T
-
-    sent = pl.ds(K, slots - K)
-    pltpu.make_async_remote_copy(
-        src_ref=send.at[sent], dst_ref=recv.at[sent], send_sem=send_sem,
-        recv_sem=recv_sem.at[0], device_id=to(1), device_id_type=MESH,
-    ).wait_send()
-    if not later:
-        for q in range(n_sys):
-            @pl.when(q != my_sys)
             def _():
                 share_copy(my_sys, q).wait_send()
 
@@ -327,19 +360,22 @@
     variations = response.shape[1]
     vmem = pl.BlockSpec(memory_space=pltpu.VMEM)
     hbm = pl.BlockSpec(memory_space=pltpu.HBM)
-    slots = n_ev * K
+    slots = n_ev * PITCH
     results = (
         jax.ShapeDtypeStruct((variations, B), F32),
         jax.ShapeDtypeStruct((1, B), F32),
     )
     scratch = [
-        pltpu.VMEM((slots, variations), F32),
-        pltpu.VMEM((slots, variations), F32),
+        pltpu.VMEM((n_ev, PITCH, variations), F32),
+        pltpu.VMEM((n_ev, PITCH, variations), F32),
         pltpu.VMEM((n_ev, 1, 128), F32),
         pltpu.VMEM((n_ev, 1, 128), F32),
         pltpu.VMEM((B, slots), BF16),
+        pltpu.VMEM((1, B), F32),
         pltpu.SemaphoreType.DMA,
         pltpu.SemaphoreType.DMA((ARRIVALS,)),
+        pltpu.SemaphoreType.DMA,
+        pltpu.SemaphoreType.DMA,
         pltpu.SemaphoreType.DMA,
         pltpu.SemaphoreType.DMA,
     ]

time: 24.6 us -> 24.3 us (0.988)
  Pallas kernels: 23.8 us -> 23.5 us
    pallas_call x1, Pallas kernels: 23.1 us -> 22.8 us  [local(): pl.pallas_call(functools.partial(exchange, n_ev, n_sys, False), out_shape...]
where the time goes in v3:
time: 24.3 us; the launch traced here: 24.2 us
  Pallas kernels  23.5 us (97%)
  between operations  0.68 us (3%)
    pallas_call x1, Pallas kernels, local(): pl.pallas_call(functools.partial(exchange, n_ev, n_sys, False), out_shape...  22.8 us
    pallas_call x1, Pallas kernels, finish(): pl.pallas_call(store, out_shape=(jax.ShapeDtypeStruct((1,) + templates.sh...  0.68 us

profile of v3, /device:TPU:1, one launch (start us, length us, event | category | flops | bytes accessed | tf_op | source)
XLA Modules:
  0.0 24.2 jit_solution(13121387927005007939)
XLA Ops:
  0.6 22.8 %first_round.1 = (f32[128,256]{1,0:T(8,128)S(1)}, f32[1,256]{1,0:T(1,128)S(1)}, f32[1,64]{1,0:T(1,128)S(1)}, f32[512,128]{1,0:T(8,128)S(1)}, f32[8,512]{1,0:T(8,128)S(1)}) custom-call(bf16[512,512]{1,0:T(8,128)(2,1)} %refs_0_.1, s32[512,512]{1,0:T(8,128)} %refs_1_.1, f32[1,512]{1,0:T(1,128)} %bitcast.10, s32[1,512]{1,0:T(1,128)} %bitcast.11, ...), custom_call_target="tpu_custom_call" | custom-call | tf_op jit(solution)/shard_map/first_round/pallas_call | solution.py:382
  23.5 0.7 %store.1 = (f32[1,128,256]{2,1,0:T(8,128)}, f32[1,256]{1,0:T(1,128)}) custom-call(f32[128,256]{1,0:T(8,128)S(1)} %get-tuple-element.48.hist_ref, f32[1,256]{1,0:T(1,128)S(1)} %get-tuple-element.49.expected_ref), custom_call_target="tpu_custom_call" | custom-call | tf_op jit(solution)/shard_map/store/pallas_call | solution.py:345
  (1 shorter events, 0.0 us)

commit v4 on v3

--- a/solution.py
+++ b/solution.py
@@ -12,9 +12,8 @@
 PITCH = 32
 SECOND_LANE = 32
 N_LANE = 64
-STRIDE = 27
 PACKS = 8
-FIRST_PACKS = 8
+FIRST_PACKS = 7
 ARRIVALS = 4
 STEPS = 4
 VMEM_BYTES = 48 << 20
@@ -48,10 +47,17 @@
     return lax.dot_general(a, b, (((1,), (1,)), ((), ())), preferred_element_type=F32)
 
 
-def far(i):
-    away = STRIDE * i % 64
-    x, z, y = away // 2 % 4, away // 8 % 2, away // 16
-    return -(min(x, 4 - x) + z + min(y, 4 - y))
+SIZES = (2, 4, 2, 4)
+PLACES = sorted(range(64), key=lambda d: (d != 0, -sum(min(e, n - e) for e, n in zip(
+    (d // 2 % 4, d // 8 % 2, d // 16), (4, 2, 4))), d % 2, d * 27 % 64))
+
+
+def digits(position):
+    out = []
+    for size in SIZES:
+        out.append(position % size)
+        position = position // size
+    return out
 
 
 def prepare(n_ev, me, hbm_refs, weight, info, vmem_refs, small_sem, load_sem, greet):
@@ -82,8 +88,13 @@
     for copy in small:
         copy.wait()
     cat = cat_ref[...]
-    away = jnp.where(cat < me, cat - me + n_ev, cat - me)
-    block = away * pow(STRIDE, -1, n_ev) % n_ev
+    away, stride = 0, 1
+    for digit, own, size in zip(digits(cat), digits(me), SIZES):
+        away = away + (digit - own + size) % size * stride
+        stride = stride * size
+    at = iota((8, n_ev), 1)
+    order = sum(jnp.where(at == place, i, 0) for i, place in enumerate(PLACES))
+    block = dot(order.astype(F32).astype(BF16), onehot(iota((n_ev, events), 0) == away))[0:1].astype(jnp.int32)
     in_block = iota((n_ev, events), 0) == block
     ahead = dot(onehot(in_block), before)
     rank = jnp.sum(jnp.where(in_block, ahead, 0.0), axis=0, keepdims=True)
@@ -92,8 +103,13 @@
     info[1:2, :] = rank
     info[2:3, :] = bin_ref[...].astype(F32)
     info[3:4, :] = base
-    base_col = jnp.broadcast_to(base, (variations, events)).T
-
+    return loads
+
+
+def weigh(loads, weight, info, obs, sel, resp_ref):
+    events, variations = weight.shape
+    rows = events // STEPS
+    base_col = jnp.broadcast_to(info[3:4, :], (variations, events)).T
     for i in range(STEPS):
         part = pl.ds(i * rows, rows)
         for load in loads[i]:
@@ -127,9 +143,13 @@
     first_half = my_sys < half
     partner = n_sys - 1 - my_sys
 
+    shifted, stride = [], 1
+    for own, size in zip(digits(me), SIZES):
+        shifted.append([lax.rem(own + e, size) * stride for e in range(size)])
+        stride = stride * size
+
     def to(i):
-        peer = me + STRIDE * i % n_ev
-        return {"ev": jnp.where(peer >= n_ev, peer - n_ev, peer)}
+        return {"ev": sum(values[e] for values, e in zip(shifted, digits(PLACES[i])))}
 
     def greet():
         if later:
@@ -142,7 +162,7 @@
                 def _():
                     pl.semaphore_signal(barrier, inc=1, device_id={"sys": q}, device_id_type=MESH)
 
-        for i in sorted(range(1, n_ev), key=far):
+        for i in range(1, n_ev):
             pl.semaphore_signal(barrier, inc=1, device_id=to(i), device_id_type=MESH)
 
     def share_copy(sender, target):
@@ -158,28 +178,15 @@
     recv[:, K:, :] = jnp.zeros((n_ev, PITCH - K, variations), F32)
     if later:
         greet()
-        pl.semaphore_wait(barrier, n_ev - 1 + jnp.where(first_half, 1, 0))
     else:
         pull_copy = pltpu.make_async_copy(pull_hbm, pull_ref, small_sem.at[4])
         pull_copy.start()
+
         @pl.when(my_sys >= half)
         def _():
             share[0:half] = jnp.zeros((half, 1, events), F32)
 
-        prepare(n_ev, me, hbm_refs, weight, info, vmem_refs, small_sem, load_sem, greet)
-
-        pull_copy.wait()
-        var_at = iota((variations, variations // 2), 0)
-        mine = iota((variations, variations // 2), 1) == var_at // 2
-        pull = jnp.sum(jnp.where(mine, pull_ref[...], 0.0), axis=1, keepdims=True)
-        odd = iota((variations, 1), 0) % 2
-        coef = jnp.maximum(jnp.where(odd == 0, pull, -pull), 0.0)
-        share[my_sys] = jnp.sum(coef * (weight[...].T - info[3:4, :]), axis=0, keepdims=True)
-        pl.semaphore_wait(barrier, n_ev - 1 + jnp.where(first_half, half - 1, n_sys - 1))
-        for q in range(n_sys):
-            @pl.when(jnp.logical_and(q != my_sys, jnp.logical_or(my_sys >= half, q < half)))
-            def _():
-                share_copy(my_sys, q).start()
+        loads = prepare(n_ev, me, hbm_refs, weight, info, vmem_refs, small_sem, load_sem, greet)
 
     block = info[0:1, :].astype(jnp.int32)
     rank_f = info[1:2, :]
@@ -195,16 +202,29 @@
     tags = dot_nt(jnp.where(in_block, info[2:3, :], 0.0).astype(BF16), at_place)
     tags = jnp.where(iota(tags.shape, 1) >= N_LANE, most, tags)
 
+    if not later:
+        weigh(loads, weight, info, vmem_refs[0], vmem_refs[1], vmem_refs[5])
+
+        pull_copy.wait()
+        var_at = iota((variations, variations // 2), 0)
+        mine = iota((variations, variations // 2), 1) == var_at // 2
+        pull = jnp.sum(jnp.where(mine, pull_ref[...], 0.0), axis=1, keepdims=True)
+        odd = iota((variations, 1), 0) % 2
+        coef = jnp.maximum(jnp.where(odd == 0, pull, -pull), 0.0)
+        share[my_sys] = jnp.sum(coef * (weight[...].T - info[3:4, :]), axis=0, keepdims=True)
+
     halves = jnp.concatenate(parts(weight[...], 2), axis=1)
     blocks = n_ev // PACKS
     count = blocks * PITCH
 
-    def pack(p):
+    def fill(p):
         pick = onehot(iota((count, events), 0) + p * count == slot)
         both = dot(pick, halves)
         both = (both[:, :variations] + both[:, variations:]).reshape(blocks, PITCH, variations)
         tag = tags[p * blocks : (p + 1) * blocks, None, :]
         send[pl.ds(p * blocks, blocks)] = jnp.where(iota(both.shape, 1) == K, tag, both)
+
+    def ship(p):
         for i in range(p * blocks, (p + 1) * blocks):
             if i > 0:
                 pltpu.make_async_remote_copy(
@@ -216,8 +236,20 @@
                     device_id_type=MESH,
                 ).start()
 
-    for p in range(FIRST_PACKS):
-        pack(p)
+    if later:
+        pl.semaphore_wait(barrier, n_ev - 1 + jnp.where(first_half, 1, 0))
+    else:
+        pl.semaphore_wait(barrier, n_ev - 1 + jnp.where(first_half, half - 1, n_sys - 1))
+        for q in range(n_sys):
+            @pl.when(jnp.logical_and(q != my_sys, jnp.logical_or(my_sys >= half, q < half)))
+            def _():
+                share_copy(my_sys, q).start()
+
+    fill(0)
+    ship(0)
+    for p in range(1, FIRST_PACKS):
+        fill(p)
+        ship(p)
     recv[0, :, :] = send[0, :, :]
 
     if not later:
@@ -247,7 +279,8 @@
         terms_copy(i, i).start()
     terms_in[0] = terms[0]
     for p in range(FIRST_PACKS, PACKS):
-        pack(p)
+        fill(p)
+        ship(p)
 
     blocks = n_ev // ARRIVALS
     count = blocks * PITCH

time: 24.3 us -> 24.1 us (level)
  no operation moved by 1% of the time
where the time goes in v4:
time: 24.1 us; the launch traced here: 24 us
  Pallas kernels  23.3 us (97%)
  between operations  0.68 us (3%)
    pallas_call x1, Pallas kernels, local(): pl.pallas_call(functools.partial(exchange, n_ev, n_sys, False), out_shape...  22.6 us
    pallas_call x1, Pallas kernels, finish(): pl.pallas_call(store, out_shape=(jax.ShapeDtypeStruct((1,) + templates.sh...  0.68 us

profile of v4, /device:TPU:1, one launch (start us, length us, event | category | flops | bytes accessed | tf_op | source)
XLA Modules:
  0.0 24.0 jit_solution(11051933415448293983)
XLA Ops:
  0.6 22.6 %first_round.1 = (f32[128,256]{1,0:T(8,128)S(1)}, f32[1,256]{1,0:T(1,128)S(1)}, f32[1,64]{1,0:T(1,128)S(1)}, f32[512,128]{1,0:T(8,128)S(1)}, f32[8,512]{1,0:T(8,128)S(1)}) custom-call(bf16[512,512]{1,0:T(8,128)(2,1)} %refs_0_.1, s32[512,512]{1,0:T(8,128)} %refs_1_.1, f32[1,512]{1,0:T(1,128)} %bitcast.10, s32[1,512]{1,0:T(1,128)} %bitcast.11, ...), custom_call_target="tpu_custom_call" | custom-call | tf_op jit(solution)/shard_map/first_round/pallas_call | solution.py:415
  23.3 0.7 %store.1 = (f32[1,128,256]{2,1,0:T(8,128)}, f32[1,256]{1,0:T(1,128)}) custom-call(f32[128,256]{1,0:T(8,128)S(1)} %get-tuple-element.48.hist_ref, f32[1,256]{1,0:T(1,128)S(1)} %get-tuple-element.49.expected_ref), custom_call_target="tpu_custom_call" | custom-call | tf_op jit(solution)/shard_map/store/pallas_call | solution.py:378
  (1 shorter events, 0.0 us)

commit v5 on v4

--- a/solution.py
+++ b/solution.py
@@ -14,7 +14,7 @@
 N_LANE = 64
 PACKS = 8
 FIRST_PACKS = 7
-ARRIVALS = 4
+ARRIVALS = 8
 STEPS = 4
 VMEM_BYTES = 48 << 20
 MESH = pl.DeviceIdType.MESH
@@ -291,7 +291,7 @@
     spread = onehot(jnp.logical_and(iota((128, count), 0) == place, used))
 
     def flat(rows):
-        spaced = dot(rows, spread).reshape(-1, blocks, count)
+        spaced = dot(rows.astype(BF16), spread).reshape(-1, blocks, count)
         return jnp.sum(jnp.where(ours[None], spaced, 0.0), axis=1)
 
     def arrived(a):
@@ -302,7 +302,7 @@
             send_sem=send_sem, recv_sem=recv_sem.at[a], device_id=to(1), device_id_type=MESH,
         ).wait_recv()
         tag = recv[pl.ds(first, blocks), K, :]
-        bins = jnp.where(used, flat(tag.astype(BF16)), -1.0).astype(jnp.int32)
+        bins = jnp.where(used, flat(tag), -1.0).astype(jnp.int32)
         in_bin = onehot(iota((B, count), 0) == bins)
         picked[:, a * count : (a + 1) * count] = in_bin
         rows = recv[pl.ds(first, blocks)].reshape(count, variations)
@@ -320,7 +320,7 @@
     got = terms_in[:, 0, :]
     pieces = parts(got, 2) + parts(pltpu.roll(got, 128 - SECOND_LANE, axis=1), 2)
     lanes = [
-        flat(jnp.concatenate([piece[a * blocks : (a + 1) * blocks] for piece in pieces], axis=0))
+        flat(jnp.concatenate([piece.astype(F32)[a * blocks : (a + 1) * blocks] for piece in pieces], axis=0))
         for a in range(ARRIVALS)
     ]
     lanes = jnp.concatenate([jnp.concatenate(lanes, axis=1), jnp.zeros((4, slots), F32)], axis=0)

time: 24.1 us -> 24.1 us (level)
  no operation moved by 1% of the time
where the time goes in v5:
time: 24.1 us; the launch traced here: 24 us
  Pallas kernels  23.3 us (97%)
  between operations  0.68 us (3%)
    pallas_call x1, Pallas kernels, local(): pl.pallas_call(functools.partial(exchange, n_ev, n_sys, False), out_shape...  22.6 us
    pallas_call x1, Pallas kernels, finish(): pl.pallas_call(store, out_shape=(jax.ShapeDtypeStruct((1,) + templates.sh...  0.68 us

profile of v5, /device:TPU:1, one launch (start us, length us, event | category | flops | bytes accessed | tf_op | source)
XLA Modules:
  0.0 24.0 jit_solution(2946016338138044742)
XLA Ops:
  0.6 22.6 %first_round.1 = (f32[128,256]{1,0:T(8,128)S(1)}, f32[1,256]{1,0:T(1,128)S(1)}, f32[1,64]{1,0:T(1,128)S(1)}, f32[512,128]{1,0:T(8,128)S(1)}, f32[8,512]{1,0:T(8,128)S(1)}) custom-call(bf16[512,512]{1,0:T(8,128)(2,1)} %refs_0_.1, s32[512,512]{1,0:T(8,128)} %refs_1_.1, f32[1,512]{1,0:T(1,128)} %bitcast.10, s32[1,512]{1,0:T(1,128)} %bitcast.11, ...), custom_call_target="tpu_custom_call" | custom-call | tf_op jit(solution)/shard_map/first_round/pallas_call | solution.py:415
  23.3 0.7 %store.1 = (f32[1,128,256]{2,1,0:T(8,128)}, f32[1,256]{1,0:T(1,128)}) custom-call(f32[128,256]{1,0:T(8,128)S(1)} %get-tuple-element.48.hist_ref, f32[1,256]{1,0:T(1,128)S(1)} %get-tuple-element.49.expected_ref), custom_call_target="tpu_custom_call" | custom-call | tf_op jit(solution)/shard_map/store/pallas_call | solution.py:378
  (1 shorter events, 0.0 us)
